TPU v7x, 32 devices: a whole 2x2x4 slice. The times are simulated.
32 devices in a mesh: dom: 4 (over y, x), fsdp: 8 (over z, core).
Axes of the slice: x: 2, y: 2, z: 4, core: 2. Of those that a mesh axis runs over, the one named last changes fastest.
Arguments:
- inputs: bfloat16 [4, 1024, 4096], P('dom', 'fsdp'), may hold values from -6 to 6
- cotangent: bfloat16 [4, 1024, 8192], P('dom', 'fsdp'), may hold values from -6 to 6
- shared_weight: bfloat16 [4096, 8192], P(None, 'fsdp'), may hold values from -0.09375 to 0.09375
- domain_weight: bfloat16 [4, 4096, 8192], P('dom', None, 'fsdp'), may hold values from 0.099609375 to 1.8984375
- row_counts: int32 [4], P('dom'), may hold values from 65 to 1024, as said below
Outputs:
- shared_grad: float32 [4096, 8192], P('dom', 'fsdp')
- domain_grad: bfloat16 [4, 4096, 8192], P('dom', None, 'fsdp')
- input_grad: bfloat16 [4, 1024, 4096], P('dom', 'fsdp')
Inputs may be any that keep to these rules, and one draw needn't show every extreme that they name: `row_counts`: rows of a domain at positions from its count on are padding. Some domain is full in every draw.
All inputs are finite; a program needn't handle non-finite values.
Results may differ from a plain program's by a relative error of at most 0.017.
Values may be sent and summed in bfloat16 or wider, within the bound.
A program may use at most 128 MiB of HBM per device.

v0:
```python
import jax
import jax.numpy as jnp
from jax import lax
from jax.sharding import PartitionSpec as P


def body(inputs, cotangent, shared_weight, domain_weight, row_counts):
    effective = (shared_weight.astype(jnp.float32) * domain_weight[0].astype(jnp.float32)).astype(
        jnp.bfloat16
    )
    live_rows = row_counts[0]
    columns = lax.all_to_all(cotangent[0], "fsdp", split_axis=1, concat_axis=0, tiled=True)
    piece = lax.all_gather(inputs[0], "fsdp", axis=0, tiled=True)
    length = piece.shape[0]
    upstream = columns.astype(jnp.float32)
    preact = jnp.dot(piece, effective, preferred_element_type=jnp.float32)
    sigma = jax.nn.sigmoid(preact)
    position = lax.iota(jnp.int32, length)
    slope = upstream * sigma * (1.0 + preact * (1.0 - sigma))
    fold_grad_pre = jnp.where((position < live_rows)[:, None], slope, jnp.float32(0.0)).astype(
        jnp.bfloat16
    )
    weight_sum = lax.dot_general(
        piece, fold_grad_pre, (((0,), (0,)), ((), ())), preferred_element_type=jnp.float32
    )
    weight_sum, grad_pre = (weight_sum, fold_grad_pre)
    scaled = weight_sum * lax.rsqrt(live_rows.astype(jnp.float32))
    input_grad = lax.psum_scatter(
        lax.dot_general(
            grad_pre, effective, (((1,), (1,)), ((), ())), preferred_element_type=jnp.float32
        ).astype(jnp.bfloat16),
        "fsdp",
        scatter_dimension=0,
        tiled=True,
    )
    shared_grad = lax.psum_scatter(
        (scaled * domain_weight[0].astype(jnp.float32)).astype(jnp.bfloat16),
        "dom",
        scatter_dimension=0,
        tiled=True,
    ).astype(jnp.float32)
    domain_grad = (scaled * shared_weight.astype(jnp.float32)).astype(jnp.bfloat16)
    return (shared_grad, domain_grad[None], input_grad[None])


def solution(mesh):
    return jax.shard_map(
        body,
        mesh=mesh,
        in_specs=(
            P("dom", "fsdp", None),
            P("dom", "fsdp", None),
            P(None, "fsdp"),
            P("dom", None, "fsdp"),
            P("dom"),
        ),
        out_specs=(P("dom", "fsdp"), P("dom", None, "fsdp"), P("dom", "fsdp", None)),
        check_vma=False,
    )
```

profile of v0, /device:TPU:0, one launch (start us, length us, event | category | flops | bytes accessed | tf_op | source)
XLA Modules:
  0.0 358.8 jit_solution(8678285528174618740)
XLA Ops:
  7.2 0.0 all-gather.3.cloned.1.call-start
  7.2 0.7 all-gather.3.cloned.1.call-update
  7.9 4.1 %copy.13 = bf16[1,128,8192]{1,2,0:T(8,128)(2,1)} copy(bf16[1,128,8192]{2,1,0:T(8,128)(2,1)} %param.6) | data formatting | bytes 4194304 | tf_op args[1]
  12.0 6.4 %all-to-all-start = ((bf16[128,8,1024]{0,2,1:T(8,128)(2,1)}), bf16[128,8,1024]{0,2,1:T(8,128)(2,1)S(1)}, u32[]{:S(2)}, u32[]{:S(2)}) async-start(bf16[128,8,1024]{0,2,1:T(8,128)(2,1)} %bitcast.1), calls=%async_computation | async-start | bytes 4194304 | tf_op jit(solution)/shard_map/all_to_all | solution.py:12
  18.3 0.0 reduce-scatter.3.cloned.1.call-start
  19.1 11.3 %copy.15 = bf16[4096,1024]{0,1:T(8,128)(2,1)} copy(bf16[4096,1024]{1,0:T(8,128)(2,1)} %param.7) | data formatting | bytes 16777216 | tf_op args[2]
  30.4 11.3 %copy.16 = bf16[1,4096,1024]{1,2,0:T(8,128)(2,1)} copy(bf16[1,4096,1024]{2,1,0:T(8,128)(2,1)} %param.8) | data formatting | bytes 16777216 | tf_op args[3]
  41.6 81.1 %all-to-all-done = bf16[128,8,1024]{0,2,1:T(8,128)(2,1)S(1)} async-done(((bf16[128,8,1024]{0,2,1:T(8,128)(2,1)}), bf16[128,8,1024]{0,2,1:T(8,128)(2,1)S(1)}, u32[]{:S(2)}, u32[]{:S(2)}) %all-to-all-start) | async-done | bytes 2097184 | tf_op jit(solution)/shard_map/all_to_all | solution.py:12
  122.7 13.7 %all-gather.3.cloned.1.call-done = bf16[1,1024,4096]{2,1,0:T(8,128)(2,1)} async-done(((bf16[1,128,4096]{2,1,0:T(8,128)(2,1)}), bf16[1,1024,4096]{2,1,0:T(8,128)(2,1)}) %all-gather.3.cloned.1.call-update) | async-done | bytes 8388624 | tf_op jit(solution)/shard_map/all_gather | solution.py:13
  136.4 17.1 %fusion.10 = bf16[1024,1024]{0,1:T(8,128)(2,1)} fusion(bf16[1,1024,4096]{2,1,0:T(8,128)(2,1)} %all-gather.3.cloned.1.call-done, bf16[4096,1024]{0,1:T(8,128)(2,1)} %copy.15, bf16[1,4096,1024]{1,2,0:T(8,128)(2,1)} %copy.16, pred[1024]{0:T(1024)(128)(4,1)S(1)} %iota_compare_fusion, bf16[128,8,1024]{0,2,1:T(8,128)(2,1)S(1)} %all-to-all-done), kind=kOutput, calls=%fused_computation.15 | convolution fusion | flops 8618246144 | bytes 29361152 | tf_op jit(solution)/shard_map/dot_general | solution.py:16
  153.5 20.9 %fusion.3 = (bf16[1,4096,1024]{1,2,0:T(8,128)(2,1)}, bf16[4096,1024]{0,1:T(8,128)(2,1)}) fusion(bf16[4096,1024]{0,1:T(8,128)(2,1)} %copy.15, f32[]{:T(128)S(6)} %rsqrt.3, bf16[1,4096,1024]{1,2,0:T(8,128)(2,1)} %copy.16, bf16[1024,1024]{0,1:T(8,128)(2,1)} %fusion.10, bf16[1,1024,4096]{2,1,0:T(8,128)(2,1)} %all-gather.3.cloned.1.call-done), kind=kOutput, calls=%fused_computation.6 | convolution fusion | flops 8619294720 | bytes 44040196 | tf_op jit(solution)/shard_map/dot_general | solution.py:23
  174.4 0.0 copy-start
  174.4 0.0 reduce-scatter.3.cloned.1.call-update
  174.5 0.2 reduce-scatter.5.cloned.1.call-start
  174.7 1.3 copy-done
  176.0 17.8 %convolution_convert_fusion = bf16[1024,4096]{1,0:T(8,128)(2,1)} fusion(bf16[1024,1024]{0,1:T(8,128)(2,1)S(1)} %copy-done, bf16[4096,1024]{0,1:T(8,128)(2,1)} %copy.15, bf16[1,4096,1024]{1,2,0:T(8,128)(2,1)} %copy.16), kind=kOutput, calls=%fused_computation.11 | convolution fusion | flops 8610906112 | bytes 27262976 | tf_op jit(solution)/shard_map/dot_general | solution.py:29
  193.8 0.0 reduce-scatter.5.cloned.1.call-update
  193.9 12.0 %copy.18 = bf16[1,4096,1024]{2,1,0:T(8,128)(2,1)} copy(bf16[1,4096,1024]{1,2,0:T(8,128)(2,1)} %get-tuple-element.9) | data formatting | bytes 16777216
  205.9 54.0 %reduce-scatter.3.cloned.1.call-done = bf16[1024,1024]{0,1:T(8,128)(2,1)} async-done(((bf16[4096,1024]{0,1:T(8,128)(2,1)}), bf16[1024,1024]{0,1:T(8,128)(2,1)}) %reduce-scatter.3.cloned.1.call-update) | async-done | bytes 2097168 | tf_op jit(solution)/shard_map/reduce_scatter | solution.py:36
  259.8 4.1 %copy.17 = f32[1024,1024]{1,0:T(8,128)} copy(bf16[1024,1024]{0,1:T(8,128)(2,1)} %reduce-scatter.3.cloned.1.call-done) | data formatting | bytes 6291456
  263.9 88.3 %reduce-scatter.5.cloned.1.call-done = bf16[128,4096]{1,0:T(8,128)(2,1)} async-done(((bf16[1024,4096]{1,0:T(8,128)(2,1)}), bf16[128,4096]{1,0:T(8,128)(2,1)}) %reduce-scatter.5.cloned.1.call-update) | async-done | bytes 1048592 | tf_op jit(solution)/shard_map/reduce_scatter | solution.py:28
  (1 shorter events, 0.0 us)
Async XLA Ops:
  7.2 129.2 %all-gather.3.cloned.1.call-start = ((), (), s32[]{:S(2)}) async-start(), calls=%async_computation.5 | async-start | bytes 9437184 | tf_op jit(solution)/shard_map/all_gather | solution.py:13
  12.0 110.8 %all-to-all-start = ((bf16[128,8,1024]{0,2,1:T(8,128)(2,1)}), bf16[128,8,1024]{0,2,1:T(8,128)(2,1)S(1)}, u32[]{:S(2)}, u32[]{:S(2)}) async-start(bf16[128,8,1024]{0,2,1:T(8,128)(2,1)} %bitcast.1), calls=%async_computation | async-start | bytes 4194304 | tf_op jit(solution)/shard_map/all_to_all | solution.py:12
  18.3 241.5 %reduce-scatter.3.cloned.1.call-start = ((), (), s32[]{:S(2)}) async-start(), calls=%async_computation.3 | async-start | bytes 10485760 | tf_op jit(solution)/shard_map/reduce_scatter | solution.py:36
  174.4 1.6 copy-start
  174.5 177.8 %reduce-scatter.5.cloned.1.call-start = ((), (), s32[]{:S(2)}) async-start(), calls=%async_computation.4 | async-start | bytes 9437184 | tf_op jit(solution)/shard_map/reduce_scatter | solution.py:28
Sparse Core Ops, SparseCore 0:
  9.6 126.7 all-gather.2
  174.6 85.2 reduce-scatter.2
  262.7 89.5 reduce-scatter.4
where the time goes:
time: 360 us; the launch traced here: 359 us
  waiting for transfers between devices  238 us (66%)
  matrix products  55.8 us (16%)
  local copies, waits for them, and re-layouts  44.1 us (12%)
  between operations  14.4 us (4%)
  starting transfers between devices  6.65 us (2%)
    reduce_scatter x1, waiting for transfers between devices, body(): lax.psum_scatter(lax.dot_general(grad_pre, effective, (((1,), (1,)), ((),...  88.3 us
    all_to_all x1, waiting for transfers between devices, body(): lax.all_to_all(cotangent[0], 'fsdp', split_axis=1, concat_axis=0, tiled=T...  81.1 us
    reduce_scatter x1, waiting for transfers between devices, body(): lax.psum_scatter((scaled * domain_weight[0].astype(jnp.float32)).astype(j...  54 us
    unnamed x7, local copies, waits for them, and re-layouts  44.1 us
    dot_general x1, matrix products, body(): lax.dot_general(piece, fold_grad_pre, (((0,), (0,)), ((), ())), preferred...  20.9 us
    dot_general x1, matrix products, body(): lax.dot_general(grad_pre, effective, (((1,), (1,)), ((), ())), preferred_...  17.8 us
    dot_general x1, matrix products, body(): preact = jnp.dot(piece, effective, preferred_element_type=jnp.float32)  17.1 us
    all_gather x1, waiting for transfers between devices, body(): piece = lax.all_gather(inputs[0], 'fsdp', axis=0, tiled=True)  13.7 us
  transfers between devices with their start and end apart: 4, of which 4 were waited for; matrix products, arithmetic and copies ran while one was open for 17% of the time, Pallas kernels for 0%

commit v1 on v0

v1 whole, which is shorter than its diff:
```python
import functools

import jax
import jax.numpy as jnp
from jax import lax
from jax.experimental import pallas as pl
from jax.experimental.pallas import tpu as pltpu
from jax.sharding import PartitionSpec as P

MESH = pl.DeviceIdType.MESH
F32 = jnp.float32
BF16 = jnp.bfloat16


def entry_barrier(axis, me, n):
    barrier = pltpu.get_barrier_semaphore()

    def greet(k, carry):
        pl.semaphore_signal(
            barrier, inc=1, device_id={axis: lax.rem(me + k, n)}, device_id_type=MESH
        )
        return carry

    lax.fori_loop(1, n, greet, 0)
    pl.semaphore_wait(barrier, n - 1)


def first_kernel(
    n, x_ref, g_ref, sw_ref, dw_ref, count_ref, x_out, gp_out, dx_out,
    xs, gs, gp, dx, weff, swb, dwb,
    up_sem, down_sem, side_sem, x_sem, gsend_sem, g_sem, load_sem, own_sem, out_sem,
):
    me = lax.axis_index("fsdp")
    nz = n // 2
    z, c = lax.div(me, 2), lax.rem(me, 2)
    rows, depth = x_ref.shape
    width = sw_ref.shape[1]
    tile = swb.shape[1]

    entry_barrier("fsdp", me, n)

    def slot(buf, chip, core):
        return buf.at[chip, pl.ds(pl.multiple_of(core * rows, rows), rows)]

    def x_copy(src, chip, core, sem, target):
        return pltpu.make_async_remote_copy(
            src_ref=src,
            dst_ref=slot(xs, chip, core),
            send_sem=sem.at[chip],
            recv_sem=x_sem.at[chip * 2 + core],
            device_id={"fsdp": target},
            device_id_type=MESH,
        )

    def g_copy(target):
        cols = pl.ds(pl.multiple_of(target * width, width), width)
        return pltpu.make_async_remote_copy(
            src_ref=g_ref.at[:, cols],
            dst_ref=slot(gs, z, c),
            send_sem=gsend_sem.at[target],
            recv_sem=g_sem.at[me],
            device_id={"fsdp": target},
            device_id_type=MESH,
        )

    up, down, sibling = me + 2, me - 2, z * 2 + (1 - c)

    @pl.when(z + 1 < nz)
    def _():
        x_copy(x_ref, z, c, up_sem, up).start()

    @pl.when(z > 0)
    def _():
        x_copy(x_ref, z, c, down_sem, down).start()

    x_copy(x_ref, z, c, side_sem, sibling).start()

    def send_g(k, carry):
        g_copy(lax.rem(me + k, n)).start()
        return carry

    lax.fori_loop(1, n, send_g, 0)

    own_x = pltpu.make_async_copy(x_ref, slot(xs, z, c), own_sem.at[0])
    own_g = pltpu.make_async_copy(
        g_ref.at[:, pl.ds(pl.multiple_of(me * width, width), width)], slot(gs, z, c), own_sem.at[1]
    )
    own_x.start()
    own_g.start()

    def load(i, b):
        at = pl.ds(pl.multiple_of(i * tile, tile), tile)
        return (
            pltpu.make_async_copy(sw_ref.at[at], swb.at[b], load_sem.at[b, 0]),
            pltpu.make_async_copy(dw_ref.at[at], dwb.at[b], load_sem.at[b, 1]),
        )

    tiles = depth // tile
    for copy in load(0, 0):
        copy.start()

    def make_weff(i, carry):
        b = lax.rem(i, 2)

        @pl.when(i + 1 < tiles)
        def _():
            for copy in load(i + 1, 1 - b):
                copy.start()

        for copy in load(i, b):
            copy.wait()
        at = pl.ds(pl.multiple_of(i * tile, tile), tile)
        weff[at, :] = (swb[b].astype(F32) * dwb[b].astype(F32)).astype(BF16)
        return carry

    lax.fori_loop(0, tiles, make_weff, 0)
    own_x.wait()
    own_g.wait()

    count = count_ref[0]
    wt = min(256, width)
    dt = min(512, depth)

    def out_copies(chip):
        return (
            pltpu.make_async_copy(xs.at[chip], x_out.at[chip], out_sem.at[chip, 0]),
            pltpu.make_async_copy(gp.at[chip], gp_out.at[chip], out_sem.at[chip, 1]),
            pltpu.make_async_copy(dx.at[chip], dx_out.at[chip], out_sem.at[chip, 2]),
        )

    def receive(chip, distance, forward, target, sem):
        @pl.when(distance > 0)
        def _():
            x_copy(slot(xs, chip, c), chip, c, side_sem, sibling).wait_recv()

            @pl.when(forward)
            def _():
                x_copy(slot(xs, chip, c), chip, c, sem, target).start()

            x_copy(slot(xs, chip, c), chip, c, side_sem, sibling).start()

    def compute(chip, distance):
        pltpu.make_async_remote_copy(
            src_ref=slot(xs, chip, 1 - c),
            dst_ref=slot(xs, chip, 1 - c),
            send_sem=side_sem.at[chip],
            recv_sem=x_sem.at[chip * 2 + 1 - c],
            device_id={"fsdp": sibling},
            device_id_type=MESH,
        ).wait_recv()
        copies = out_copies(chip)
        copies[0].start()

        def wait_g(core):
            pltpu.make_async_remote_copy(
                src_ref=slot(gs, chip, core),
                dst_ref=slot(gs, chip, core),
                send_sem=gsend_sem.at[me],
                recv_sem=g_sem.at[chip * 2 + core],
                device_id={"fsdp": sibling},
                device_id_type=MESH,
            ).wait_recv()

        wait_g(1 - c)

        @pl.when(distance > 0)
        def _():
            wait_g(c)

        def pre(i, carry):
            at = pl.ds(pl.multiple_of(i * wt, wt), wt)
            preact = jnp.dot(xs[chip], weff[:, at], preferred_element_type=F32)
            sigma = jax.nn.sigmoid(preact)
            position = chip * (2 * rows) + lax.broadcasted_iota(jnp.int32, preact.shape, 0)
            slope = gs[chip, :, at].astype(F32) * sigma * (1.0 + preact * (1.0 - sigma))
            gp[chip, :, at] = jnp.where(position < count, slope, 0.0).astype(BF16)
            return carry

        lax.fori_loop(0, width // wt, pre, 0)
        copies[1].start()

        def back(i, carry):
            at = pl.ds(pl.multiple_of(i * dt, dt), dt)
            dx[chip, :, at] = lax.dot_general(
                gp[chip], weff[at, :], (((1,), (1,)), ((), ())), preferred_element_type=F32
            ).astype(BF16)
            return carry

        lax.fori_loop(0, depth // dt, back, 0)
        copies[2].start()

    def step(distance, carry):
        below, above = z - distance, z + distance
        has_below = (below >= 0) & (distance > 0)
        has_above = above < nz

        @pl.when(has_below)
        def _():
            receive(below, distance, z + 1 < nz, up, up_sem)

        @pl.when(has_above)
        def _():
            receive(above, distance, z > 0, down, down_sem)

        @pl.when(has_below)
        def _():
            compute(below, distance)

        @pl.when(has_above)
        def _():
            compute(above, distance)

        return carry

    lax.fori_loop(0, nz, step, 0)

    def finish(chip, carry):
        @pl.when((chip <= z) & (z + 1 < nz))
        def _():
            x_copy(slot(xs, chip, c), chip, c, up_sem, up).wait_send()

        @pl.when((chip >= z) & (z > 0))
        def _():
            x_copy(slot(xs, chip, c), chip, c, down_sem, down).wait_send()

        x_copy(slot(xs, chip, c), chip, c, side_sem, sibling).wait_send()
        for copy in out_copies(chip):
            copy.wait()
        return carry

    lax.fori_loop(0, nz, finish, 0)

    def finish_g(k, carry):
        g_copy(lax.rem(me + k, n)).wait_send()
        return carry

    lax.fori_loop(1, n, finish_g, 0)


def forward_and_input_grad(n, x, g, sw, dw, count):
    rows, depth = x.shape
    width = sw.shape[1]
    nz = n // 2
    tile = min(256, depth)
    whole = jax.ShapeDtypeStruct((nz, 2 * rows, depth), BF16)
    cols = jax.ShapeDtypeStruct((nz, 2 * rows, width), BF16)
    any_spec = pl.BlockSpec(memory_space=pl.ANY)
    dma = pltpu.SemaphoreType.DMA
    return pl.pallas_call(
        functools.partial(first_kernel, n),
        out_shape=(whole, cols, whole),
        in_specs=[any_spec] * 4 + [pl.BlockSpec(memory_space=pltpu.SMEM)],
        out_specs=(any_spec,) * 3,
        scratch_shapes=[
            pltpu.VMEM(whole.shape, BF16),
            pltpu.VMEM(cols.shape, BF16),
            pltpu.VMEM(cols.shape, BF16),
            pltpu.VMEM(whole.shape, BF16),
            pltpu.VMEM((depth, width), BF16),
            pltpu.VMEM((2, tile, width), BF16),
            pltpu.VMEM((2, tile, width), BF16),
            dma((nz,)),
            dma((nz,)),
            dma((nz,)),
            dma((n,)),
            dma((n,)),
            dma((n,)),
            dma((2, 2)),
            dma((2,)),
            dma((nz, 3)),
        ],
        compiler_params=pltpu.CompilerParams(
            collective_id=0, has_side_effects=True, vmem_limit_bytes=60 * 1024 * 1024
        ),
        name="gather_and_backprop",
    )(x, g, sw, dw, count)


def solution(mesh):
    n = mesh.shape["fsdp"]

    def body(inputs, cotangent, shared_weight, domain_weight, row_counts):
        live_rows = row_counts[0]
        piece, grad_pre, partial = forward_and_input_grad(
            n, inputs[0], cotangent[0], shared_weight, domain_weight[0], row_counts
        )
        depth = piece.shape[-1]
        piece = piece.reshape(-1, depth)
        grad_pre = grad_pre.reshape(piece.shape[0], -1)
        partial = partial.reshape(-1, depth)
        input_grad = lax.psum_scatter(partial, "fsdp", scatter_dimension=0, tiled=True)
        weight_sum = lax.dot_general(
            piece, grad_pre, (((0,), (0,)), ((), ())), preferred_element_type=F32
        )
        scaled = weight_sum * lax.rsqrt(live_rows.astype(F32))
        shared_grad = lax.psum_scatter(
            (scaled * domain_weight[0].astype(F32)).astype(BF16),
            "dom",
            scatter_dimension=0,
            tiled=True,
        ).astype(F32)
        domain_grad = (scaled * shared_weight.astype(F32)).astype(BF16)
        return (shared_grad, domain_grad[None], input_grad[None])

    return jax.shard_map(
        body,
        mesh=mesh,
        in_specs=(
            P("dom", "fsdp", None),
            P("dom", "fsdp", None),
            P(None, "fsdp"),
            P("dom", None, "fsdp"),
            P("dom"),
        ),
        out_specs=(P("dom", "fsdp"), P("dom", None, "fsdp"), P("dom", "fsdp", None)),
        check_vma=False,
    )
```

time: 360 us -> 348 us (0.967)
  Pallas kernels: 0 us -> 130 us
  waiting for transfers between devices: 238 us -> 176 us
  local copies, waits for them, and re-layouts: 44.1 us -> 0 us
  matrix products: 55.8 us -> 22.9 us
  starting transfers between devices: 6.65 us -> 0.08 us
  other arithmetic: 0.01 us -> 4.07 us
    pallas_call x0 -> x1, Pallas kernels: none -> 130 us  [forward_and_input_grad(): pl.pallas_call(functools.partial(first_kernel, n), out_shape=(whole, cols...]
    all_to_all x1 -> x0, waiting for transfers between devices: 81.1 us -> none  [body(): lax.all_to_all(cotangent[0], 'fsdp', split_axis=1, concat_axis=0, tiled=T...]
    unnamed x7 -> x0, local copies, waits for them, and re-layouts: 44.1 us -> none
    reduce_scatter x2, waiting for transfers between devices: 142 us -> 175 us  [the longest x1 88.4 us: body(): lax.psum_scatter(partial, 'fsdp', scatter_dimension=0, tiled=True)]
    dot_general x3 -> x1, matrix products: 55.8 us -> 22.9 us  [body(): lax.dot_general(piece, grad_pre, (((0,), (0,)), ((), ())), preferred_elem...]
    all_gather x1 -> x0, waiting for transfers between devices: 13.7 us -> none  [body(): piece = lax.all_gather(inputs[0], 'fsdp', axis=0, tiled=True)]
    all_to_all x1 -> x0, starting transfers between devices: 6.35 us -> none  [body(): lax.all_to_all(cotangent[0], 'fsdp', split_axis=1, concat_axis=0, tiled=T...]
    convert_element_type x0 -> x1, other arithmetic: none -> 4.07 us  [body(): shared_grad = lax.psum_scatter((scaled * domain_weight[0].astype(F32)).as...]
  transfers between devices with their start and end apart: 4 -> 2, of which waited for: 4 -> 2; matrix products, arithmetic and copies ran while one was open for 17% -> 1% of each run, Pallas kernels for 0% -> 0%
where the time goes in v1:
time: 348 us
  waiting for transfers between devices  176 us (51%)
  Pallas kernels  130 us (37%)
  matrix products  22.9 us (7%)
  between operations  14.7 us (4%)
  other arithmetic  4.07 us (1%)
    pallas_call x1, Pallas kernels, forward_and_input_grad(): pl.pallas_call(functools.partial(first_kernel, n), out_shape=(whole, cols...  130 us
    reduce_scatter x1, waiting for transfers between devices, body(): lax.psum_scatter(partial, 'fsdp', scatter_dimension=0, tiled=True)  88.4 us
    reduce_scatter x1, waiting for transfers between devices, body(): lax.psum_scatter((scaled * domain_weight[0].astype(F32)).astype(BF16), 'd...  86.9 us
    dot_general x1, matrix products, body(): lax.dot_general(piece, grad_pre, (((0,), (0,)), ((), ())), preferred_elem...  22.9 us
  transfers between devices with their start and end apart: 2, of which 2 were waited for; matrix products, arithmetic and copies ran while one was open for 1% of the time, Pallas kernels for 0%

profile of v1, /device:TPU:0, one launch (start us, length us, event | category | flops | bytes accessed | tf_op | source)
XLA Modules:
  0.0 348.0 jit_solution(5912824053668382922)
XLA Ops:
  7.2 0.0 reduce-scatter.3.cloned.1.call-start
  7.9 130.2 %gather_and_backprop.1 = (bf16[4,256,4096]{2,1,0:T(8,128)(2,1)}, bf16[4,256,1024]{2,1,0:T(8,128)(2,1)}, bf16[4,256,4096]{2,1,0:T(8,128)(2,1)}) custom-call(bf16[128,4096]{1,0:T(8,128)(2,1)} %bitcast.22, bf16[128,8192]{1,0:T(8,128)(2,1)} %bitcast.21, bf16[4096,1024]{1,0:T(8,128)(2,1)} %sw_ref.1, bf16[4096,1024]{1,0:T(8,128)(2,1)} %bitcast.19, ...), custom_call_target="tpu_custom_call" | custom-call | tf_op jit(solution)/shard_map/gather_and_backprop/pallas_call | solution.py:249
  138.1 22.9 %fusion = (bf16[1,4096,1024]{2,1,0:T(8,128)(2,1)}, bf16[4096,1024]{1,0:T(8,128)(2,1)}) fusion(bf16[4096,1024]{1,0:T(8,128)(2,1)} %sw_ref.1, f32[]{:T(128)} %bitcast.4, bf16[1,4096,1024]{2,1,0:T(8,128)(2,1)} %param.8, bf16[4,256,4096]{2,1,0:T(8,128)(2,1)} %get-tuple-element.6, bf16[4,256,1024]{2,1,0:T(8,128)(2,1)} %get-tuple-element.7), kind=kOutput, calls=%fused_computation.3 | convolution fusion | flops 8619294720 | bytes 44040196 | tf_op jit(solution)/shard_map/dot_general | solution.py:292
  161.1 0.0 reduce-scatter.3.cloned.1.call-update
  161.1 0.0 reduce-scatter.5.cloned.1.call-start
  161.2 0.7 reduce-scatter.5.cloned.1.call-update
  161.9 86.9 %reduce-scatter.3.cloned.1.call-done = bf16[1024,1024]{1,0:T(8,128)(2,1)} async-done(((bf16[4096,1024]{1,0:T(8,128)(2,1)}), bf16[1024,1024]{1,0:T(8,128)(2,1)}) %reduce-scatter.3.cloned.1.call-update) | async-done | bytes 2097168 | tf_op jit(solution)/shard_map/reduce_scatter | solution.py:296
  248.8 4.1 %convert_element_type.22 = f32[1024,1024]{1,0:T(8,128)} convert(bf16[1024,1024]{1,0:T(8,128)(2,1)} %reduce-scatter.3.cloned.1.call-done) | non-fusion elementwise | flops 1048576 | bytes 6291456 | tf_op jit(solution)/shard_map/convert_element_type | solution.py:301
  252.8 88.4 %reduce-scatter.5.cloned.1.call-done = bf16[128,4096]{1,0:T(8,128)(2,1)} async-done(((bf16[1024,4096]{1,0:T(8,128)(2,1)}), bf16[128,4096]{1,0:T(8,128)(2,1)}) %reduce-scatter.5.cloned.1.call-update) | async-done | bytes 1048592 | tf_op jit(solution)/shard_map/reduce_scatter | solution.py:291
Async XLA Ops:
  7.2 241.6 %reduce-scatter.3.cloned.1.call-start = ((), (), s32[]{:S(2)}) async-start(), calls=%async_computation.2 | async-start | bytes 10485760 | tf_op jit(solution)/shard_map/reduce_scatter | solution.py:296
  161.1 180.1 %reduce-scatter.5.cloned.1.call-start = ((), (), s32[]{:S(2)}) async-start(), calls=%async_computation.3 | async-start | bytes 9437184 | tf_op jit(solution)/shard_map/reduce_scatter | solution.py:291
Sparse Core Ops, SparseCore 0:
  161.2 87.4 reduce-scatter.2
  251.6 89.5 reduce-scatter.4

commit v2 on v1

--- a/solution.py
+++ b/solution.py
@@ -276,30 +276,359 @@
     )(x, g, sw, dw, count)
 
 
+def second_kernel(
+    n, nd, x_ref, gp_ref, dx_ref, sw_ref, dw_ref, count_ref, shared_out, dom_out, in_out,
+    xv, gv, tb, rb, acc, sib, chain, swb,
+    load_sem, acc_sem, sib_send, sib_recv, ch_send, ch_recv, d_send, d_recv, sw_sem, dw_sem, out_sem,
+):
+    me, dom = lax.axis_index("fsdp"), lax.axis_index("dom")
+    nz = n // 2
+    z, c = lax.div(me, 2), lax.rem(me, 2)
+    sibling = z * 2 + (1 - c)
+    bits = nd.bit_length() - 1
+    parts = min(2, bits)
+    rows = in_out.shape[0]
+    width = gv.shape[1]
+    half = width // parts
+    block = shared_out.shape[0]
+    tile = min(256, block)
+    pieces = block // tile
+
+    def flip(value, mask):
+        for b in range(bits):
+            if mask >> b & 1:
+                value = value + (1 << b) - (2 << b) * lax.rem(lax.div(value, 1 << b), 2)
+        return value
+
+    barrier = pltpu.get_barrier_semaphore()
+    for b in range(bits):
+        pl.semaphore_signal(
+            barrier, inc=1, device_id={"dom": flip(dom, 1 << b)}, device_id_type=MESH
+        )
+    for near in (lax.rem(me + 2, n), lax.rem(me + n - 2, n), sibling):
+        pl.semaphore_signal(barrier, inc=1, device_id={"fsdp": near}, device_id_type=MESH)
+    pl.semaphore_wait(barrier, bits + 3)
+
+    load_x = pltpu.make_async_copy(x_ref, xv, load_sem.at[0])
+    load_g = pltpu.make_async_copy(gp_ref, gv, load_sem.at[1])
+    load_x.start()
+    load_g.start()
+
+    order = sorted(range(nd), key=lambda m: (-bin(m).count("1"), m))
+
+    def bit_order(p):
+        return [(p + s) % bits for s in range(bits)]
+
+    def sent_at(m, p):
+        return next((s for s, b in enumerate(bit_order(p)) if m >> b & 1), bits)
+
+    index = {}
+    for p in range(parts):
+        for m in range(1, nd):
+            s = sent_at(m, p)
+            index[p, s, m ^ (1 << bit_order(p)[s])] = len(index)
+
+    def block_rows(m, q):
+        return pl.ds(pl.multiple_of(flip(dom, m) * block + q * tile, tile), tile)
+
+    def part(p):
+        return pl.ds(p * half, half)
+
+    def piece_rows(q):
+        return pl.ds(pl.multiple_of(q * tile, tile), tile)
+
+    def d_copy(m, p, q):
+        s = sent_at(m, p)
+        bit = 1 << bit_order(p)[s]
+        at = index[p, s, m ^ bit]
+        return pltpu.make_async_remote_copy(
+            src_ref=tb.at[block_rows(m, q), part(p)],
+            dst_ref=rb.at[at, piece_rows(q)],
+            send_sem=d_send.at[at, q],
+            recv_sem=d_recv.at[at, q],
+            device_id={"dom": flip(dom, bit)},
+            device_id_type=MESH,
+        )
+
+    def arrived(m, p, q, steps):
+        total = tb[block_rows(m, q), part(p)].astype(F32)
+        for s in range(steps):
+            at = index[p, s, m]
+            pltpu.make_async_remote_copy(
+                src_ref=rb.at[at, piece_rows(q)],
+                dst_ref=rb.at[at, piece_rows(q)],
+                send_sem=d_send.at[at, q],
+                recv_sem=d_recv.at[at, q],
+                device_id={"dom": flip(dom, 1 << bit_order(p)[s])},
+                device_id_type=MESH,
+            ).wait_recv()
+            total = total + rb[at, piece_rows(q), :].astype(F32)
+        return total
+
+    def whole_block(m):
+        return pl.ds(pl.multiple_of(flip(dom, m) * block, block), block)
+
+    def sw_load(i):
+        return pltpu.make_async_copy(
+            sw_ref.at[whole_block(order[i])], swb.at[i % 2], sw_sem.at[i]
+        )
+
+    def dw_load(i):
+        at = whole_block(order[i])
+        return pltpu.make_async_copy(dw_ref.at[at], tb.at[at], dw_sem.at[i])
+
+    def dom_store(i):
+        return pltpu.make_async_copy(
+            swb.at[i % 2], dom_out.at[whole_block(order[i])], out_sem.at[i]
+        )
+
+    sw_load(0).start()
+    for i in range(nd):
+        dw_load(i).start()
+
+    def own_rows(chip):
+        return dx_ref.at[chip, pl.ds(pl.multiple_of(c * rows, rows), rows)]
+
+    def acc_load(chip):
+        return pltpu.make_async_copy(own_rows(chip), acc.at[chip], acc_sem.at[chip])
+
+    def sib_copy(chip):
+        return pltpu.make_async_remote_copy(
+            src_ref=dx_ref.at[chip, pl.ds(pl.multiple_of((1 - c) * rows, rows), rows)],
+            dst_ref=sib.at[chip],
+            send_sem=sib_send.at[chip],
+            recv_sem=sib_recv.at[chip],
+            device_id={"fsdp": sibling},
+            device_id_type=MESH,
+        )
+
+    def chain_copy(slot, chip, target):
+        return pltpu.make_async_remote_copy(
+            src_ref=acc.at[chip],
+            dst_ref=chain.at[slot],
+            send_sem=ch_send.at[chip],
+            recv_sem=ch_recv.at[slot],
+            device_id={"fsdp": target},
+            device_id_type=MESH,
+        )
+
+    def send_up(chip):
+        return chain_copy(chip, chip, lax.rem(me + 2, n))
+
+    def send_down(chip):
+        slot = jnp.where(chip == z - 1, nz, chip)
+        return chain_copy(slot, chip, lax.rem(me + n - 2, n))
+
+    def start_sib(chip, carry):
+        sib_copy(chip).start()
+        acc_load(chip).start()
+        return carry
+
+    lax.fori_loop(0, nz, start_sib, 0)
+
+    scale = lax.rsqrt(jnp.full((1, 1), count_ref[0], jnp.int32).astype(F32))
+    load_x.wait()
+    load_g.wait()
+
+    def weight_block(i):
+        m = order[i]
+        if i + 1 < nd:
+            if i >= 1:
+                dom_store(i - 1).wait()
+            sw_load(i + 1).start()
+        sw_load(i).wait()
+        dw_load(i).wait()
+
+        def one(q, carry):
+            at = block_rows(m, q)
+            scaled = scale * lax.dot_general(
+                xv[:, at], gv[...], (((0,), (0,)), ((), ())), preferred_element_type=F32
+            )
+            tb[at, :] = (scaled * tb[at, :].astype(F32)).astype(BF16)
+            for p in range(parts):
+                if sent_at(m, p) == 0:
+                    d_copy(m, p, q).start()
+            here = piece_rows(q)
+            swb[i % 2, here, :] = (scaled * swb[i % 2, here, :].astype(F32)).astype(BF16)
+            return carry
+
+        lax.fori_loop(0, pieces, one, 0)
+        dom_store(i).start()
+
+    weight_block(0)
+
+    def pair_sum(k, carry):
+        def add(chip):
+            acc_load(chip).wait()
+            sib_copy(chip).wait_recv()
+            acc[chip] = (acc[chip].astype(F32) + sib[chip].astype(F32)).astype(BF16)
+
+        chip = jnp.where(z == 0, nz - 1 - k, k)
+        add(chip)
+
+        @pl.when((z == 0) & (chip > z))
+        def _():
+            send_up(chip).start()
+
+        @pl.when((z == nz - 1) & (chip < z))
+        def _():
+            send_down(chip).start()
+
+        return carry
+
+    lax.fori_loop(0, nz, pair_sum, 0)
+
+    for i in range(1, nd):
+        weight_block(i)
+
+    for s in range(1, bits):
+        for m in order:
+            for p in range(parts):
+                if m and sent_at(m, p) == s:
+
+                    def relay(q, carry, m=m, p=p, s=s):
+                        total = arrived(m, p, q, s).astype(BF16)
+                        tb[block_rows(m, q), part(p)] = total
+                        d_copy(m, p, q).start()
+                        return carry
+
+                    lax.fori_loop(0, pieces, relay, 0)
+
+    def hop(t, carry):
+        def take(slot, chip):
+            pltpu.make_async_remote_copy(
+                src_ref=chain.at[slot],
+                dst_ref=chain.at[slot],
+                send_sem=ch_send.at[chip],
+                recv_sem=ch_recv.at[slot],
+                device_id={"fsdp": sibling},
+                device_id_type=MESH,
+            ).wait_recv()
+            acc[chip] = (acc[chip].astype(F32) + chain[slot].astype(F32)).astype(BF16)
+
+        rising = nz - 1 - (t - z)
+        falling = t - (nz - 1 - z)
+
+        @pl.when((z > 0) & (t >= z))
+        def _():
+            take(rising, rising)
+
+            @pl.when(rising > z)
+            def _():
+                send_up(rising).start()
+
+        @pl.when((z < nz - 1) & (falling >= 0))
+        def _():
+            take(jnp.where(falling == z, nz, falling), falling)
+
+            @pl.when(falling < z)
+            def _():
+                send_down(falling).start()
+
+        return carry
+
+    lax.fori_loop(1, nz - 1, hop, 0)
+
+    def final(q, carry):
+        for p in range(parts):
+            shared_out[piece_rows(q), part(p)] = arrived(0, p, q, bits)
+        return carry
+
+    lax.fori_loop(0, pieces, final, 0)
+    if nz > 1:
+        hop(nz - 1, 0)
+    in_out[...] = acc[z]
+
+    for i in range(max(0, nd - 2), nd):
+        dom_store(i).wait()
+    for m in range(1, nd):
+        for p in range(parts):
+
+            def drain(q, carry, m=m, p=p):
+                d_copy(m, p, q).wait_send()
+                return carry
+
+            lax.fori_loop(0, pieces, drain, 0)
+
+    def drain_chain(chip, carry):
+        sib_copy(chip).wait_send()
+
+        @pl.when(chip > z)
+        def _():
+            send_up(chip).wait_send()
+
+        @pl.when(chip < z)
+        def _():
+            send_down(chip).wait_send()
+
+        return carry
+
+    lax.fori_loop(0, nz, drain_chain, 0)
+
+
+def weight_grads(n, nd, x, gp, dx, sw, dw, count):
+    depth, width = sw.shape
+    total = x.shape[0]
+    rows = total // n
+    nz = n // 2
+    bits = nd.bit_length() - 1
+    parts = min(2, bits)
+    block = depth // nd
+    pieces = block // min(256, block)
+    buffers = parts * (nd - 1)
+    any_spec = pl.BlockSpec(memory_space=pl.ANY)
+    vmem_spec = pl.BlockSpec(memory_space=pltpu.VMEM)
+    dma = pltpu.SemaphoreType.DMA
+    return pl.pallas_call(
+        functools.partial(second_kernel, n, nd),
+        out_shape=(
+            jax.ShapeDtypeStruct((block, width), F32),
+            jax.ShapeDtypeStruct((depth, width), BF16),
+            jax.ShapeDtypeStruct((rows, depth), BF16),
+        ),
+        in_specs=[any_spec] * 5 + [pl.BlockSpec(memory_space=pltpu.SMEM)],
+        out_specs=(vmem_spec, any_spec, vmem_spec),
+        scratch_shapes=[
+            pltpu.VMEM((total, depth), BF16),
+            pltpu.VMEM((total, width), BF16),
+            pltpu.VMEM((depth, width), BF16),
+            pltpu.VMEM((buffers, block, width // parts), BF16),
+            pltpu.VMEM((nz, rows, depth), BF16),
+            pltpu.VMEM((nz, rows, depth), BF16),
+            pltpu.VMEM((nz + 1, rows, depth), BF16),
+            pltpu.VMEM((2, block, width), BF16),
+            dma((2,)),
+            dma((nz,)),
+            dma((nz,)),
+            dma((nz,)),
+            dma((nz,)),
+            dma((nz + 1,)),
+            dma((buffers, pieces)),
+            dma((buffers, pieces)),
+            dma((nd,)),
+            dma((nd,)),
+            dma((nd,)),
+        ],
+        compiler_params=pltpu.CompilerParams(
+            collective_id=1, has_side_effects=True, vmem_limit_bytes=62 * 1024 * 1024
+        ),
+        name="weight_grads",
+    )(x, gp, dx, sw, dw, count)
+
+
 def solution(mesh):
-    n = mesh.shape["fsdp"]
+    n, nd = mesh.shape["fsdp"], mesh.shape["dom"]
 
     def body(inputs, cotangent, shared_weight, domain_weight, row_counts):
-        live_rows = row_counts[0]
         piece, grad_pre, partial = forward_and_input_grad(
             n, inputs[0], cotangent[0], shared_weight, domain_weight[0], row_counts
         )
         depth = piece.shape[-1]
         piece = piece.reshape(-1, depth)
         grad_pre = grad_pre.reshape(piece.shape[0], -1)
-        partial = partial.reshape(-1, depth)
-        input_grad = lax.psum_scatter(partial, "fsdp", scatter_dimension=0, tiled=True)
-        weight_sum = lax.dot_general(
-            piece, grad_pre, (((0,), (0,)), ((), ())), preferred_element_type=F32
-        )
-        scaled = weight_sum * lax.rsqrt(live_rows.astype(F32))
-        shared_grad = lax.psum_scatter(
-            (scaled * domain_weight[0].astype(F32)).astype(BF16),
-            "dom",
-            scatter_dimension=0,
-            tiled=True,
-        ).astype(F32)
-        domain_grad = (scaled * shared_weight.astype(F32)).astype(BF16)
+        shared_grad, domain_grad, input_grad = weight_grads(
+            n, nd, piece, grad_pre, partial, shared_weight, domain_weight[0], row_counts
+        )
         return (shared_grad, domain_grad[None], input_grad[None])
 
     return jax.shard_map(

time: 348 us -> 236 us (0.68)
  waiting for transfers between devices: 176 us -> 0 us
  Pallas kernels: 130 us -> 221 us
  matrix products: 22.9 us -> 0 us
  local copies, waits for them, and re-layouts: 0 us -> 13.6 us
  between operations: 14.7 us -> 1.3 us
  other arithmetic: 4.07 us -> 0 us
    reduce_scatter x2 -> x0, waiting for transfers between devices: 175 us -> none  [the longest x1 88.4 us: body(): lax.psum_scatter(partial, 'fsdp', scatter_dimension=0, tiled=True)]
    pallas_call x0 -> x1, Pallas kernels: none -> 90.7 us  [weight_grads(): pl.pallas_call(functools.partial(second_kernel, n, nd), out_shape=(jax.Sh...]
    dot_general x1 -> x0, matrix products: 22.9 us -> none  [body(): lax.dot_general(piece, grad_pre, (((0,), (0,)), ((), ())), preferred_elem...]
    unnamed x0 -> x5, local copies, waits for them, and re-layouts: none -> 13.6 us
    convert_element_type x1 -> x0, other arithmetic: 4.07 us -> none  [body(): shared_grad = lax.psum_scatter((scaled * domain_weight[0].astype(F32)).as...]
  transfers between devices with their start and end apart: 2 -> 0, of which waited for: 2 -> 0; matrix products, arithmetic and copies ran while one was open for 1% -> 0% of each run, Pallas kernels for 0% -> 0%
where the time goes in v2:
time: 236 us
  Pallas kernels  221 us (94%)
  local copies, waits for them, and re-layouts  13.6 us (6%)
    pallas_call x1, Pallas kernels, forward_and_input_grad(): pl.pallas_call(functools.partial(first_kernel, n), out_shape=(whole, cols...  130 us
    pallas_call x1, Pallas kernels, weight_grads(): pl.pallas_call(functools.partial(second_kernel, n, nd), out_shape=(jax.Sh...  90.7 us
    unnamed x5, local copies, waits for them, and re-layouts  13.6 us

profile of v2, /device:TPU:0, one launch (start us, length us, event | category | flops | bytes accessed | tf_op | source)
XLA Modules:
  0.0 235.9 jit_solution(623903837470119225)
XLA Ops:
  1.3 130.2 %gather_and_backprop.1 = (bf16[4,256,4096]{2,1,0:T(8,128)(2,1)}, bf16[4,256,1024]{2,1,0:T(8,128)(2,1)}, bf16[4,256,4096]{2,1,0:T(8,128)(2,1)}) custom-call(bf16[128,4096]{1,0:T(8,128)(2,1)} %bitcast.13, bf16[128,8192]{1,0:T(8,128)(2,1)} %bitcast.12, bf16[4096,1024]{1,0:T(8,128)(2,1)} %sw_ref.3, bf16[4096,1024]{1,0:T(8,128)(2,1)} %bitcast.7, s32[1]{0:T(128)S(6)} %copy.11.count_ref), custom_call_target="tpu_custom_call" | custom-call | tf_op jit(solution)/shard_map/gather_and_backprop/pallas_call | solution.py:249
  131.5 90.7 %weight_grads.1 = (f32[1024,1024]{1,0:T(8,128)}, bf16[4096,1024]{1,0:T(8,128)(2,1)}, bf16[128,4096]{1,0:T(8,128)(2,1)}) custom-call(bf16[1024,4096]{1,0:T(8,128)(2,1)} %bitcast.9, bf16[1024,1024]{1,0:T(8,128)(2,1)} %bitcast.11, bf16[4,256,4096]{2,1,0:T(8,128)(2,1)} %get-tuple-element.11.dx_ref, bf16[4096,1024]{1,0:T(8,128)(2,1)} %sw_ref.3, ...), custom_call_target="tpu_custom_call" | custom-call | tf_op jit(solution)/shard_map/weight_grads/pallas_call | solution.py:582
  222.3 4.8 %copy.12 = f32[1024,1024]{1,0:T(8,128)} copy(f32[1024,1024]{1,0:T(8,128)} %get-tuple-element.18) | data formatting | bytes 8388608
  227.0 0.0 copy-start
  227.0 7.8 %copy.13 = bf16[1,4096,1024]{2,1,0:T(8,128)(2,1)} copy(bf16[1,4096,1024]{2,1,0:T(8,128)(2,1)} %bitcast.10) | data formatting | bytes 16777216
  234.9 0.0 copy-done
  234.9 1.0 copy.14
Async XLA Ops:
  227.0 7.8 %copy-start = (bf16[128,4096]{1,0:T(8,128)(2,1)S(1)}, bf16[128,4096]{1,0:T(8,128)(2,1)}, u32[]{:S(2)}) copy-start(bf16[128,4096]{1,0:T(8,128)(2,1)} %get-tuple-element.14) | copy-start | bytes 3145732

commit v3 on v2

--- a/solution.py
+++ b/solution.py
@@ -75,11 +75,20 @@
 
     x_copy(x_ref, z, c, side_sem, sibling).start()
 
-    def send_g(k, carry):
-        g_copy(lax.rem(me + k, n)).start()
-        return carry
-
-    lax.fori_loop(1, n, send_g, 0)
+    g_copy(sibling).start()
+
+    def send_g(distance, carry):
+        @pl.when(z - distance >= 0)
+        def _():
+            for core in range(2):
+                g_copy((z - distance) * 2 + core).start()
+
+        @pl.when(z + distance < nz)
+        def _():
+            for core in range(2):
+                g_copy((z + distance) * 2 + core).start()
+
+        return carry
 
     own_x = pltpu.make_async_copy(x_ref, slot(xs, z, c), own_sem.at[0])
     own_g = pltpu.make_async_copy(
@@ -202,13 +211,17 @@
         def _():
             receive(above, distance, z > 0, down, down_sem)
 
-        @pl.when(has_below)
-        def _():
-            compute(below, distance)
-
-        @pl.when(has_above)
-        def _():
-            compute(above, distance)
+        @pl.when(distance == 1)
+        def _():
+            lax.fori_loop(1, nz, send_g, 0)
+
+        @pl.when((below + 1 >= 0) & (distance > 1) & (above - 1 < nz))
+        def _():
+            compute(above - 1, distance - 1)
+
+        @pl.when(has_below | has_above)
+        def _():
+            compute(jnp.where(has_below, below, above), distance)
 
         return carry
 
@@ -419,7 +432,11 @@
         slot = jnp.where(chip == z - 1, nz, chip)
         return chain_copy(slot, chip, lax.rem(me + n - 2, n))
 
-    def start_sib(chip, carry):
+    def pair_order(k):
+        return jnp.where(z == 0, nz - 1 - k, k)
+
+    def start_sib(k, carry):
+        chip = pair_order(k)
         sib_copy(chip).start()
         acc_load(chip).start()
         return carry
@@ -427,8 +444,6 @@
     lax.fori_loop(0, nz, start_sib, 0)
 
     scale = lax.rsqrt(jnp.full((1, 1), count_ref[0], jnp.int32).astype(F32))
-    load_x.wait()
-    load_g.wait()
 
     def weight_block(i):
         m = order[i]
@@ -455,15 +470,13 @@
         lax.fori_loop(0, pieces, one, 0)
         dom_store(i).start()
 
-    weight_block(0)
-
     def pair_sum(k, carry):
         def add(chip):
             acc_load(chip).wait()
             sib_copy(chip).wait_recv()
             acc[chip] = (acc[chip].astype(F32) + sib[chip].astype(F32)).astype(BF16)
 
-        chip = jnp.where(z == 0, nz - 1 - k, k)
+        chip = pair_order(k)
         add(chip)
 
         @pl.when((z == 0) & (chip > z))
@@ -476,23 +489,14 @@
 
         return carry
 
-    lax.fori_loop(0, nz, pair_sum, 0)
+    pair_sum(0, 0)
+    load_x.wait()
+    load_g.wait()
+    weight_block(0)
+    lax.fori_loop(1, nz, pair_sum, 0)
 
     for i in range(1, nd):
         weight_block(i)
-
-    for s in range(1, bits):
-        for m in order:
-            for p in range(parts):
-                if m and sent_at(m, p) == s:
-
-                    def relay(q, carry, m=m, p=p, s=s):
-                        total = arrived(m, p, q, s).astype(BF16)
-                        tb[block_rows(m, q), part(p)] = total
-                        d_copy(m, p, q).start()
-                        return carry
-
-                    lax.fori_loop(0, pieces, relay, 0)
 
     def hop(t, carry):
         def take(slot, chip):
@@ -527,7 +531,22 @@
 
         return carry
 
-    lax.fori_loop(1, nz - 1, hop, 0)
+    if nz > 2:
+        hop(1, 0)
+    for s in range(1, bits):
+        for m in order:
+            for p in range(parts):
+                if m and sent_at(m, p) == s:
+
+                    def relay(q, carry, m=m, p=p, s=s):
+                        total = arrived(m, p, q, s).astype(BF16)
+                        tb[block_rows(m, q), part(p)] = total
+                        d_copy(m, p, q).start()
+                        return carry
+
+                    lax.fori_loop(0, pieces, relay, 0)
+
+    lax.fori_loop(2, nz - 1, hop, 0)
 
     def final(q, carry):
         for p in range(parts):

time: 236 us -> 232 us (0.983)
  Pallas kernels: 221 us -> 217 us
    pallas_call x1, Pallas kernels: 130 us -> 119 us  [forward_and_input_grad(): pl.pallas_call(functools.partial(first_kernel, n), out_shape=(whole, cols...]
    pallas_call x1, Pallas kernels: 90.7 us -> 97.8 us  [weight_grads(): pl.pallas_call(functools.partial(second_kernel, n, nd), out_shape=(jax.Sh...]
where the time goes in v3:
time: 232 us
  Pallas kernels  217 us (94%)
  local copies, waits for them, and re-layouts  13.6 us (6%)
    pallas_call x1, Pallas kernels, forward_and_input_grad(): pl.pallas_call(functools.partial(first_kernel, n), out_shape=(whole, cols...  119 us
    pallas_call x1, Pallas kernels, weight_grads(): pl.pallas_call(functools.partial(second_kernel, n, nd), out_shape=(jax.Sh...  97.8 us
    unnamed x5, local copies, waits for them, and re-layouts  13.6 us

profile of v3, /device:TPU:0, one launch (start us, length us, event | category | flops | bytes accessed | tf_op | source)
XLA Modules:
  0.0 231.8 jit_solution(13141227153403551189)
XLA Ops:
  1.3 119.0 %gather_and_backprop.1 = (bf16[4,256,4096]{2,1,0:T(8,128)(2,1)}, bf16[4,256,1024]{2,1,0:T(8,128)(2,1)}, bf16[4,256,4096]{2,1,0:T(8,128)(2,1)}) custom-call(bf16[128,4096]{1,0:T(8,128)(2,1)} %bitcast.13, bf16[128,8192]{1,0:T(8,128)(2,1)} %bitcast.12, bf16[4096,1024]{1,0:T(8,128)(2,1)} %sw_ref.3, bf16[4096,1024]{1,0:T(8,128)(2,1)} %bitcast.7, s32[1]{0:T(128)S(6)} %copy.11.count_ref), custom_call_target="tpu_custom_call" | custom-call | tf_op jit(solution)/shard_map/gather_and_backprop/pallas_call | solution.py:262
  120.3 97.8 %weight_grads.1 = (f32[1024,1024]{1,0:T(8,128)}, bf16[4096,1024]{1,0:T(8,128)(2,1)}, bf16[128,4096]{1,0:T(8,128)(2,1)}) custom-call(bf16[1024,4096]{1,0:T(8,128)(2,1)} %bitcast.9, bf16[1024,1024]{1,0:T(8,128)(2,1)} %bitcast.11, bf16[4,256,4096]{2,1,0:T(8,128)(2,1)} %get-tuple-element.11.dx_ref, bf16[4096,1024]{1,0:T(8,128)(2,1)} %sw_ref.3, ...), custom_call_target="tpu_custom_call" | custom-call | tf_op jit(solution)/shard_map/weight_grads/pallas_call | solution.py:601
  218.2 4.8 %copy.12 = f32[1024,1024]{1,0:T(8,128)} copy(f32[1024,1024]{1,0:T(8,128)} %get-tuple-element.18) | data formatting | bytes 8388608
  222.9 0.0 copy-start
  222.9 7.8 %copy.13 = bf16[1,4096,1024]{2,1,0:T(8,128)(2,1)} copy(bf16[1,4096,1024]{2,1,0:T(8,128)(2,1)} %bitcast.10) | data formatting | bytes 16777216
  230.8 0.0 copy-done
  230.8 1.0 copy.14
Async XLA Ops:
  222.9 7.8 %copy-start = (bf16[128,4096]{1,0:T(8,128)(2,1)S(1)}, bf16[128,4096]{1,0:T(8,128)(2,1)}, u32[]{:S(2)}) copy-start(bf16[128,4096]{1,0:T(8,128)(2,1)} %get-tuple-element.14) | copy-start | bytes 3145732

commit v4 on v3

--- a/solution.py
+++ b/solution.py
@@ -198,6 +198,8 @@
         lax.fori_loop(0, depth // dt, back, 0)
         copies[2].start()
 
+    lag = jnp.where((z > 0) & (z < nz - 1), 1, 0)
+
     def step(distance, carry):
         below, above = z - distance, z + distance
         has_below = (below >= 0) & (distance > 0)
@@ -215,17 +217,19 @@
         def _():
             lax.fori_loop(1, nz, send_g, 0)
 
-        @pl.when((below + 1 >= 0) & (distance > 1) & (above - 1 < nz))
-        def _():
-            compute(above - 1, distance - 1)
-
-        @pl.when(has_below | has_above)
-        def _():
-            compute(jnp.where(has_below, below, above), distance)
-
-        return carry
-
-    lax.fori_loop(0, nz, step, 0)
+        late = distance - lag
+
+        @pl.when((late > 0) & (z - late >= 0))
+        def _():
+            compute(z - late, late)
+
+        @pl.when((late >= 0) & (z + late < nz))
+        def _():
+            compute(z + late, late)
+
+        return carry
+
+    lax.fori_loop(0, nz + 1, step, 0)
 
     def finish(chip, carry):
         @pl.when((chip <= z) & (z + 1 < nz))
@@ -635,6 +639,28 @@
     )(x, gp, dx, sw, dw, count)
 
 
+def store_kernel(a_ref, b_ref, c_ref, a_out, b_out, c_out):
+    a_out[...] = a_ref[...]
+    b_out[...] = b_ref[...]
+    c_out[...] = c_ref[...]
+
+
+def store_results(*arrays):
+    steps = 8
+    specs = tuple(
+        pl.BlockSpec((a.shape[0] // steps, a.shape[1]), lambda i: (i, 0)) for a in arrays
+    )
+    return pl.pallas_call(
+        store_kernel,
+        grid=(steps,),
+        out_shape=tuple(jax.ShapeDtypeStruct(a.shape, a.dtype) for a in arrays),
+        in_specs=specs,
+        out_specs=specs,
+        compiler_params=pltpu.CompilerParams(vmem_limit_bytes=63 * 1024 * 1024),
+        name="store_results",
+    )(*arrays)
+
+
 def solution(mesh):
     n, nd = mesh.shape["fsdp"], mesh.shape["dom"]
 
@@ -647,6 +673,9 @@
         grad_pre = grad_pre.reshape(piece.shape[0], -1)
         shared_grad, domain_grad, input_grad = weight_grads(
             n, nd, piece, grad_pre, partial, shared_weight, domain_weight[0], row_counts
+        )
+        shared_grad, domain_grad, input_grad = store_results(
+            shared_grad, domain_grad, input_grad
         )
         return (shared_grad, domain_grad[None], input_grad[None])
 

time: 232 us -> 221 us (0.953)
  local copies, waits for them, and re-layouts: 13.6 us -> 0 us
  Pallas kernels: 217 us -> 220 us
    unnamed x5 -> x0, local copies, waits for them, and re-layouts: 13.6 us -> none
    pallas_call x0 -> x1, Pallas kernels: none -> 11.7 us  [store_results(): pl.pallas_call(store_kernel, grid=(steps,), out_shape=tuple((jax.ShapeDty...]
    pallas_call x1, Pallas kernels: 97.8 us -> 88.7 us  [weight_grads(): pl.pallas_call(functools.partial(second_kernel, n, nd), out_shape=(jax.Sh...]
where the time goes in v4:
time: 221 us
  Pallas kernels  220 us (100%)
    pallas_call x1, Pallas kernels, forward_and_input_grad(): pl.pallas_call(functools.partial(first_kernel, n), out_shape=(whole, cols...  119 us
    pallas_call x1, Pallas kernels, weight_grads(): pl.pallas_call(functools.partial(second_kernel, n, nd), out_shape=(jax.Sh...  88.7 us
    pallas_call x1, Pallas kernels, store_results(): pl.pallas_call(store_kernel, grid=(steps,), out_shape=tuple((jax.ShapeDty...  11.7 us

profile of v4, /device:TPU:0, one launch (start us, length us, event | category | flops | bytes accessed | tf_op | source)
XLA Modules:
  0.0 220.8 jit_solution(6634881376262896955)
XLA Ops:
  1.3 119.0 %gather_and_backprop.1 = (bf16[4,256,4096]{2,1,0:T(8,128)(2,1)}, bf16[4,256,1024]{2,1,0:T(8,128)(2,1)}, bf16[4,256,4096]{2,1,0:T(8,128)(2,1)}) custom-call(bf16[128,4096]{1,0:T(8,128)(2,1)} %bitcast.12, bf16[128,8192]{1,0:T(8,128)(2,1)} %bitcast.11, bf16[4096,1024]{1,0:T(8,128)(2,1)} %sw_ref.3, bf16[4096,1024]{1,0:T(8,128)(2,1)} %bitcast.7, s32[1]{0:T(128)S(6)} %copy.8.count_ref), custom_call_target="tpu_custom_call" | custom-call | tf_op jit(solution)/shard_map/gather_and_backprop/pallas_call | solution.py:266
  120.3 88.7 %weight_grads.1 = (f32[1024,1024]{1,0:T(8,128)}, bf16[4096,1024]{1,0:T(8,128)(2,1)}, bf16[128,4096]{1,0:T(8,128)(2,1)}) custom-call(bf16[1024,4096]{1,0:T(8,128)(2,1)} %bitcast.9, bf16[1024,1024]{1,0:T(8,128)(2,1)} %bitcast.10, bf16[4,256,4096]{2,1,0:T(8,128)(2,1)} %get-tuple-element.14.dx_ref, bf16[4096,1024]{1,0:T(8,128)(2,1)} %sw_ref.3, ...), custom_call_target="tpu_custom_call" | custom-call | tf_op jit(solution)/shard_map/weight_grads/pallas_call | solution.py:605
  209.1 11.7 %store_results.1 = (f32[1024,1024]{1,0:T(8,128)}, bf16[4096,1024]{1,0:T(8,128)(2,1)}, bf16[128,4096]{1,0:T(8,128)(2,1)}) custom-call(f32[1024,1024]{1,0:T(8,128)} %get-tuple-element.15.a_ref, bf16[4096,1024]{1,0:T(8,128)(2,1)} %get-tuple-element.16.b_ref, bf16[128,4096]{1,0:T(8,128)(2,1)} %get-tuple-element.17.c_ref), custom_call_target="tpu_custom_call" | custom-call | tf_op jit(solution)/shard_map/store_results/pallas_call | solution.py:653

commit v5 on v4

--- a/solution.py
+++ b/solution.py
@@ -317,20 +317,6 @@
                 value = value + (1 << b) - (2 << b) * lax.rem(lax.div(value, 1 << b), 2)
         return value
 
-    barrier = pltpu.get_barrier_semaphore()
-    for b in range(bits):
-        pl.semaphore_signal(
-            barrier, inc=1, device_id={"dom": flip(dom, 1 << b)}, device_id_type=MESH
-        )
-    for near in (lax.rem(me + 2, n), lax.rem(me + n - 2, n), sibling):
-        pl.semaphore_signal(barrier, inc=1, device_id={"fsdp": near}, device_id_type=MESH)
-    pl.semaphore_wait(barrier, bits + 3)
-
-    load_x = pltpu.make_async_copy(x_ref, xv, load_sem.at[0])
-    load_g = pltpu.make_async_copy(gp_ref, gv, load_sem.at[1])
-    load_x.start()
-    load_g.start()
-
     order = sorted(range(nd), key=lambda m: (-bin(m).count("1"), m))
 
     def bit_order(p):
@@ -399,9 +385,24 @@
             swb.at[i % 2], dom_out.at[whole_block(order[i])], out_sem.at[i]
         )
 
+    def x_load(i):
+        at = whole_block(order[i])
+        return pltpu.make_async_copy(x_ref.at[:, at], xv.at[:, at], load_sem.at[i])
+
+    load_g = pltpu.make_async_copy(gp_ref, gv, load_sem.at[nd])
+    load_g.start()
+    x_load(0).start()
     sw_load(0).start()
-    for i in range(nd):
-        dw_load(i).start()
+    dw_load(0).start()
+
+    barrier = pltpu.get_barrier_semaphore()
+    for b in range(bits):
+        pl.semaphore_signal(
+            barrier, inc=1, device_id={"dom": flip(dom, 1 << b)}, device_id_type=MESH
+        )
+    for near in (lax.rem(me + 2, n), lax.rem(me + n - 2, n), sibling):
+        pl.semaphore_signal(barrier, inc=1, device_id={"fsdp": near}, device_id_type=MESH)
+    pl.semaphore_wait(barrier, bits + 3)
 
     def own_rows(chip):
         return dx_ref.at[chip, pl.ds(pl.multiple_of(c * rows, rows), rows)]
@@ -457,6 +458,7 @@
             sw_load(i + 1).start()
         sw_load(i).wait()
         dw_load(i).wait()
+        x_load(i).wait()
 
         def one(q, carry):
             at = block_rows(m, q)
@@ -493,8 +495,10 @@
 
         return carry
 
+    for i in range(1, nd):
+        x_load(i).start()
+        dw_load(i).start()
     pair_sum(0, 0)
-    load_x.wait()
     load_g.wait()
     weight_block(0)
     lax.fori_loop(1, nz, pair_sum, 0)
@@ -620,7 +624,7 @@
             pltpu.VMEM((nz, rows, depth), BF16),
             pltpu.VMEM((nz + 1, rows, depth), BF16),
             pltpu.VMEM((2, block, width), BF16),
-            dma((2,)),
+            dma((nd + 1,)),
             dma((nz,)),
             dma((nz,)),
             dma((nz,)),

time: 221 us -> 215 us (0.973)
  Pallas kernels: 220 us -> 214 us
    pallas_call x1, Pallas kernels: 88.7 us -> 82.8 us  [weight_grads(): pl.pallas_call(functools.partial(second_kernel, n, nd), out_shape=(jax.Sh...]
where the time goes in v5:
time: 215 us
  Pallas kernels  214 us (100%)
    pallas_call x1, Pallas kernels, forward_and_input_grad(): pl.pallas_call(functools.partial(first_kernel, n), out_shape=(whole, cols...  119 us
    pallas_call x1, Pallas kernels, weight_grads(): pl.pallas_call(functools.partial(second_kernel, n, nd), out_shape=(jax.Sh...  82.8 us
    pallas_call x1, Pallas kernels, store_results(): pl.pallas_call(store_kernel, grid=(steps,), out_shape=tuple((jax.ShapeDty...  11.7 us

profile of v5, /device:TPU:0, one launch (start us, length us, event | category | flops | bytes accessed | tf_op | source)
XLA Modules:
  0.0 214.9 jit_solution(10111400138759788196)
XLA Ops:
  1.3 119.0 %gather_and_backprop.1 = (bf16[4,256,4096]{2,1,0:T(8,128)(2,1)}, bf16[4,256,1024]{2,1,0:T(8,128)(2,1)}, bf16[4,256,4096]{2,1,0:T(8,128)(2,1)}) custom-call(bf16[128,4096]{1,0:T(8,128)(2,1)} %bitcast.12, bf16[128,8192]{1,0:T(8,128)(2,1)} %bitcast.11, bf16[4096,1024]{1,0:T(8,128)(2,1)} %sw_ref.3, bf16[4096,1024]{1,0:T(8,128)(2,1)} %bitcast.7, s32[1]{0:T(128)S(6)} %copy.8.count_ref), custom_call_target="tpu_custom_call" | custom-call | tf_op jit(solution)/shard_map/gather_and_backprop/pallas_call | solution.py:266
  120.3 82.8 %weight_grads.1 = (f32[1024,1024]{1,0:T(8,128)}, bf16[4096,1024]{1,0:T(8,128)(2,1)}, bf16[128,4096]{1,0:T(8,128)(2,1)}) custom-call(bf16[1024,4096]{1,0:T(8,128)(2,1)} %bitcast.9, bf16[1024,1024]{1,0:T(8,128)(2,1)} %bitcast.10, bf16[4,256,4096]{2,1,0:T(8,128)(2,1)} %get-tuple-element.14.dx_ref, bf16[4096,1024]{1,0:T(8,128)(2,1)} %sw_ref.3, ...), custom_call_target="tpu_custom_call" | custom-call | tf_op jit(solution)/shard_map/weight_grads/pallas_call | solution.py:609
  203.2 11.7 %store_results.1 = (f32[1024,1024]{1,0:T(8,128)}, bf16[4096,1024]{1,0:T(8,128)(2,1)}, bf16[128,4096]{1,0:T(8,128)(2,1)}) custom-call(f32[1024,1024]{1,0:T(8,128)} %get-tuple-element.15.a_ref, bf16[4096,1024]{1,0:T(8,128)(2,1)} %get-tuple-element.16.b_ref, bf16[128,4096]{1,0:T(8,128)(2,1)} %get-tuple-element.17.c_ref), custom_call_target="tpu_custom_call" | custom-call | tf_op jit(solution)/shard_map/store_results/pallas_call | solution.py:657
